TPU v7x, 512 devices: a whole 4x4x16 slice. The times are simulated.
512 devices in a mesh: slab: 32 (over x, y, core), pencil: 16 (over z).
Axes of the slice: x: 4, y: 4, z: 16, core: 2. Of those that a mesh axis runs over, the one named last changes fastest.
Arguments:
- orbitals: float32 [4, 192, 192, 192], P(None, 'slab', 'pencil'), may hold values from -6 to 6
- potential: float32 [192, 192, 192], P('slab', 'pencil'), may hold values from 0.5 to 2.5
- unlocked: int32 [4], replicated, may hold values 0 or 1
Outputs:
- orthonormal: float32 [4, 192, 192, 192], P(None, 'slab', 'pencil')
Inputs may be any that keep to these rules, and one draw needn't show every extreme that they name: `unlocked`: 1 marks a band that is filtered, 0 a locked band kept as it is.
All inputs are finite; a program needn't handle non-finite values.
Results may differ from a plain program's by a relative error of at most 0.00005.
Values sent between devices are 32-bit elements; how exact they have to be, the bound alone decides.
No kernel may reach another device: no remote copies, remote signals or barrier semaphores. Data moves between devices by JAX's collectives and lax.ppermute only.
A program may use at most 64 MiB of HBM per device.

v0:
```python
import math
import jax
import jax.numpy as jnp
from jax import lax
from jax.sharding import PartitionSpec as P

NG = 192
kinetic_scale = 4.0
filter_center = 1.0
filter_half = 1.5
highest = lax.Precision.HIGHEST


def frequencies(number, length):
    index = jnp.arange(number, dtype=jnp.int32)
    return jnp.where(index < length // 2, index, index - length)


def tables(number, length):
    modes = frequencies(number, length)
    places = jnp.arange(length, dtype=jnp.int32)
    product = places[:, None] * modes[None, :] % length
    angle = 2.0 * math.pi / length * product.astype(jnp.float32)
    return (jnp.cos(angle), jnp.sin(angle))


def forward_table(cosine, sine):
    return jnp.stack([jnp.stack([cosine, -sine], 1), jnp.stack([sine, cosine], 1)], 1)


def inverse_table(cosine, sine):
    cos_t = cosine.T
    sin_t = sine.T
    return jnp.stack([jnp.stack([cos_t, sin_t], 1), jnp.stack([-sin_t, cos_t], 1)], 1)


def local(orbitals, potential, unlocked):
    length = orbitals.shape[3]
    cos_k, sin_k = tables(length, length)
    cos_f, sin_f = tables(length, length)
    first_forward = jnp.stack([cos_k, -sin_k], 1)
    first_inverse = jnp.stack([cos_k.T, -sin_k.T], 1)
    second_forward = forward_table(cos_k, sin_k)
    second_inverse = inverse_table(cos_k, sin_k)
    depth_forward = forward_table(cos_f, sin_f)
    depth_inverse = inverse_table(cos_f, sin_f)
    pencil_block = length // lax.axis_size("pencil")
    slab_block = length // lax.axis_size("slab")
    kept_list = frequencies(length, length)
    third_modes = lax.dynamic_slice_in_dim(
        kept_list, lax.axis_index("pencil") * pencil_block, pencil_block
    ).astype(jnp.float32)
    second_modes = lax.dynamic_slice_in_dim(
        kept_list, lax.axis_index("slab") * slab_block, slab_block
    ).astype(jnp.float32)
    first_modes = frequencies(length, length).astype(jnp.float32)
    squared = (
        third_modes[:, None, None] ** 2
        + second_modes[None, :, None] ** 2
        + first_modes[None, None, :] ** 2
    )
    radius = float((length // 4) ** 2)
    kinetic = jnp.where(squared < radius, kinetic_scale * squared / radius, 0.0)
    lines_k = jnp.einsum("bacx,xrk->bacrk", orbitals, first_forward, precision=highest)
    along_f = jnp.einsum(
        "bacrk,crsf->baksf",
        lax.all_to_all(lines_k, "pencil", split_axis=4, concat_axis=2, tiled=True),
        second_forward,
        precision=highest,
    )
    spectra = jnp.einsum(
        "baksf,astg->bkftg",
        lax.all_to_all(along_f, "slab", split_axis=4, concat_axis=1, tiled=True),
        depth_forward,
        precision=highest,
    )
    spectra = spectra * kinetic[None, :, :, None, :]
    along_a = jnp.einsum("bkftg,gtsa->bkfsa", spectra, depth_inverse, precision=highest)
    returned = lax.all_to_all(along_a, "slab", split_axis=4, concat_axis=2, tiled=True)
    rows_c = jnp.einsum("bkfsa,fsrc->bkarc", returned, second_inverse, precision=highest)
    lines_x = lax.all_to_all(rows_c, "pencil", split_axis=4, concat_axis=1, tiled=True)
    kinetic_part = jnp.einsum("bkarc,krx->bacx", lines_x, first_inverse, precision=highest)
    kinetic_part = kinetic_part / float(NG**3)
    applied = kinetic_part + potential[None] * orbitals
    filtered = jnp.where(
        unlocked[:, None, None, None] == 1,
        (applied - filter_center * orbitals) / filter_half,
        orbitals,
    )
    number = filtered.shape[0]
    flattened = filtered.reshape(number, -1)
    partial_intersection = jnp.dot(flattened, flattened.T, precision=highest) / float(NG**3)
    intersection = lax.psum(partial_intersection, ("slab", "pencil"))
    factor = jnp.linalg.cholesky(intersection)
    result = jax.scipy.linalg.solve_triangular(factor, flattened, lower=True)
    return result.reshape(filtered.shape)


def solution(mesh):
    in_specs = (P(None, "slab", "pencil", None), P("slab", "pencil", None), P())
    out_specs = P(None, "slab", "pencil", None)
    return jax.shard_map(local, mesh=mesh, in_specs=in_specs, out_specs=out_specs, check_vma=False)
```

profile of v0, /device:TPU:1, one launch (start us, length us, event | category | flops | bytes accessed | tf_op | source)
XLA Modules:
  0.0 365.7 jit_solution(14531609065697997235)
XLA Ops:
  3.5 3.5 copy.74
  7.0 7.7 %reshape.301 = f32[16,1,6912]{2,1,0:T(1,128)} reshape(f32[192,6,2,4,12]{4,3,2,1,0:T(4,128)} %bitcast.136) | data formatting | bytes 884736
  14.7 15.9 %all-to-all-start = ((f32[16,1,6912]{2,1,0:T(1,128)}), f32[16,1,6912]{2,1,0:T(1,128)S(1)}, u32[]{:S(2)}, u32[]{:S(2)}) async-start(f32[16,1,6912]{2,1,0:T(1,128)} %reshape.301), calls=%async_computation | async-start | bytes 884736 | tf_op jit(solution)/shard_map/all_to_all | solution.py:67
  30.9 20.2 %all-to-all-done = f32[16,1,6912]{2,1,0:T(1,128)S(1)} async-done(((f32[16,1,6912]{2,1,0:T(1,128)}), f32[16,1,6912]{2,1,0:T(1,128)S(1)}, u32[]{:S(2)}, u32[]{:S(2)}) %all-to-all-start) | async-done | bytes 442400 | tf_op jit(solution)/shard_map/all_to_all | solution.py:67
  53.3 7.8 %reshape.302 = f32[192,6,2,4,12]{4,3,2,1,0:T(4,128)} reshape(f32[16,6912]{1,0:T(8,128)S(1)} %reduce.6) | data formatting | bytes 884736
  61.0 7.2 %copy.163 = f32[4,6,12,2,16,12]{2,4,3,5,1,0:T(8,128)} copy(f32[4,6,12,2,16,12]{2,0,3,1,5,4:T(4,128)} %bitcast.137) | data formatting | bytes 884736 | tf_op jit(solution)/shard_map/all_to_all | solution.py:67
  68.3 4.3 %all_to_all.55 = f32[4,6,192,2,12]{2,3,4,1,0:T(2,128)S(1)} reshape(f32[4,6,16,12,2,12]{3,2,4,5,1,0:T(8,128)} %bitcast.138) | data formatting | bytes 884736 | tf_op jit(solution)/shard_map/all_to_all | solution.py:67
  74.1 4.8 %copy.79 = f32[4,6,12,2,192]{2,3,1,0,4:T(2,128)} copy(f32[4,6,12,2,192]{4,2,3,1,0:T(8,128)S(1)} %convolution_bitcast_fusion.3) | data formatting | bytes 884736 | tf_op jit(solution)/shard_map/bacrk,crsf->baksf/dot_general | solution.py:65
  78.9 8.6 %reshape.303 = f32[32,1,3456]{2,1,0:T(1,128)} reshape(f32[192,4,6,2,12]{4,3,2,1,0:T(2,128)} %bitcast.139) | data formatting | bytes 884736
  87.5 14.1 %all-to-all-start.1 = ((f32[32,1,3456]{2,1,0:T(1,128)}), f32[32,1,3456]{2,1,0:T(1,128)S(1)}, u32[]{:S(2)}, u32[]{:S(2)}) async-start(f32[32,1,3456]{2,1,0:T(1,128)} %reshape.303), calls=%async_computation.1 | async-start | bytes 884736 | tf_op jit(solution)/shard_map/all_to_all | solution.py:73
  101.7 10.5 %all-to-all-done.1 = f32[32,1,3456]{2,1,0:T(1,128)S(1)} async-done(((f32[32,1,3456]{2,1,0:T(1,128)}), f32[32,1,3456]{2,1,0:T(1,128)S(1)}, u32[]{:S(2)}, u32[]{:S(2)}) %all-to-all-start.1) | async-done | bytes 442400 | tf_op jit(solution)/shard_map/all_to_all | solution.py:73
  113.9 8.9 %reshape.304 = f32[192,4,6,2,12]{4,3,2,1,0:T(2,128)} reshape(f32[32,3456]{1,0:T(8,128)S(1)} %reduce.7) | data formatting | bytes 884736
  122.9 6.1 %copy.81 = f32[4,32,6,12,2,6]{3,4,5,2,1,0:T(2,128)} copy(f32[4,32,6,12,2,6]{3,4,2,0,5,1:T(2,128)} %bitcast.140) | data formatting | bytes 884736 | tf_op jit(solution)/shard_map/all_to_all | solution.py:73
  129.0 6.3 %copy.107 = f32[4,192,12,2,6,1]{1,4,3,5,2,0:T(8,128)S(1)} copy(f32[4,192,12,2,6,1]{2,3,4,1,0,5:T(2,128)} %bitcast.141) | data formatting | bytes 884736 | tf_op jit(solution)/shard_map/all_to_all | solution.py:73
  135.3 3.0 fusion.1
  138.3 3.0 convolution_bitcast_fusion
  141.3 3.7 %copy.85 = f32[4,12,6,2,192]{1,0,3,2,4:T(4,128)} copy(f32[4,12,6,2,192]{4,2,3,1,0:T(8,128)S(1)} %convolution_bitcast_fusion) | data formatting | bytes 884736 | tf_op jit(solution)/shard_map/bkftg,gtsa->bkfsa/dot_general | solution.py:78
  145.0 7.2 %reshape.305 = f32[32,1,3456]{2,1,0:T(1,128)S(1)} reshape(f32[192,6,2,4,12]{4,3,2,1,0:T(4,128)} %bitcast.142) | data formatting | bytes 884736
  152.2 14.1 %all_to_all.72 = f32[32,1,3456]{2,1,0:T(1,128)S(1)} all-to-all(f32[32,1,3456]{2,1,0:T(1,128)S(1)} %reshape.305), channel_id=1, replica_groups=mesh['slab'=32,'pencil'=16] {'slab'}, dimensions={0} | all-to-all | bytes 884736 | tf_op jit(solution)/shard_map/all_to_all | solution.py:79
  168.1 7.8 %reshape.306 = f32[192,6,2,4,12]{4,3,2,1,0:T(4,128)} reshape(f32[32,3456]{1,0:T(8,128)S(1)} %reduce.8) | data formatting | bytes 884736
  175.8 4.8 %copy.86 = f32[4,12,6,2,192]{1,3,4,2,0:T(2,128)S(1)} copy(f32[4,12,6,2,192]{1,0,3,2,4:T(4,128)} %bitcast.143) | data formatting | bytes 884736 | tf_op jit(solution)/shard_map/all_to_all | solution.py:79
  180.6 3.7 %copy.87 = f32[4,12,32,6,2,6]{1,4,5,3,2,0:T(2,128)} copy(f32[4,12,32,6,2,6]{1,4,5,2,3,0:T(2,128)S(1)} %bitcast.144) | data formatting | bytes 884736 | tf_op jit(solution)/shard_map/all_to_all | solution.py:79
  184.3 6.3 %copy.113 = f32[4,12,192,2,6,1]{2,4,3,5,1,0:T(8,128)S(1)} copy(f32[4,12,192,2,6,1]{1,3,4,2,0,5:T(2,128)} %bitcast.145) | data formatting | bytes 884736 | tf_op jit(solution)/shard_map/all_to_all | solution.py:79
  190.6 3.0 convolution_bitcast_fusion.1
  193.6 3.7 %copy.90 = f32[4,12,6,2,192]{1,0,3,2,4:T(4,128)} copy(f32[4,12,6,2,192]{4,2,3,1,0:T(8,128)S(1)} %convolution_bitcast_fusion.1) | data formatting | bytes 884736 | tf_op jit(solution)/shard_map/bkfsa,fsrc->bkarc/dot_general | solution.py:80
  197.4 7.9 %reshape.307 = f32[16,1,6912]{2,1,0:T(1,128)} reshape(f32[192,6,2,4,12]{4,3,2,1,0:T(4,128)} %bitcast.146) | data formatting | bytes 884736
  205.3 5.6 %all-to-all-start.3 = ((f32[16,1,6912]{2,1,0:T(1,128)}), f32[16,1,6912]{2,1,0:T(1,128)S(1)}, u32[]{:S(2)}, u32[]{:S(2)}) async-start(f32[16,1,6912]{2,1,0:T(1,128)} %reshape.307), calls=%async_computation.3 | async-start | bytes 884736 | tf_op jit(solution)/shard_map/all_to_all | solution.py:81
  210.9 21.6 %all-to-all-done.3 = f32[16,1,6912]{2,1,0:T(1,128)S(1)} async-done(((f32[16,1,6912]{2,1,0:T(1,128)}), f32[16,1,6912]{2,1,0:T(1,128)S(1)}, u32[]{:S(2)}, u32[]{:S(2)}) %all-to-all-start.3) | async-done | bytes 442400 | tf_op jit(solution)/shard_map/all_to_all | solution.py:81
  234.2 7.8 %reshape.308 = f32[192,6,2,4,12]{4,3,2,1,0:T(4,128)} reshape(f32[16,6912]{1,0:T(8,128)S(1)} %reduce.9) | data formatting | bytes 884736
  242.0 7.2 %copy.162 = f32[4,12,6,2,16,12]{1,4,3,5,2,0:T(8,128)} copy(f32[4,12,6,2,16,12]{1,0,3,2,5,4:T(4,128)} %bitcast.147) | data formatting | bytes 884736 | tf_op jit(solution)/shard_map/all_to_all | solution.py:81
  249.2 4.4 %all_to_all.67 = f32[4,192,6,2,12]{1,3,4,2,0:T(2,128)S(1)} reshape(f32[4,16,12,6,2,12]{2,1,4,5,3,0:T(8,128)} %bitcast.148) | data formatting | bytes 884736 | tf_op jit(solution)/shard_map/all_to_all | solution.py:81
  256.1 105.4 %psum.7 = f32[4,4]{0,1:T(4,128)S(1)} all-reduce(f32[4,4]{0,1:T(4,128)S(1)} %fusion.7), channel_id=1, replica_groups=mesh['slab'=32,'pencil'=16] {'slab','pencil'}, use_global_device_ids=true, to_apply=%region_0.1 | all-reduce | flops 16 | bytes 128 | tf_op jit(solution)/shard_map/psum | solution.py:93
  (34 shorter events, 19.0 us)
Async XLA Ops:
  14.7 36.4 %all-to-all-start = ((f32[16,1,6912]{2,1,0:T(1,128)}), f32[16,1,6912]{2,1,0:T(1,128)S(1)}, u32[]{:S(2)}, u32[]{:S(2)}) async-start(f32[16,1,6912]{2,1,0:T(1,128)} %reshape.301), calls=%async_computation | async-start | bytes 884736 | tf_op jit(solution)/shard_map/all_to_all | solution.py:67
  87.5 24.7 %all-to-all-start.1 = ((f32[32,1,3456]{2,1,0:T(1,128)}), f32[32,1,3456]{2,1,0:T(1,128)S(1)}, u32[]{:S(2)}, u32[]{:S(2)}) async-start(f32[32,1,3456]{2,1,0:T(1,128)} %reshape.303), calls=%async_computation.1 | async-start | bytes 884736 | tf_op jit(solution)/shard_map/all_to_all | solution.py:73
  193.6 17.3 %copy-start.2 = (s32[4]{0:T(128)S(1)}, s32[4]{0:T(128)}, u32[]{:S(2)}) copy-start(s32[4]{0:T(128)} %param.5) | copy-start | bytes 52
  205.3 27.3 %all-to-all-start.3 = ((f32[16,1,6912]{2,1,0:T(1,128)}), f32[16,1,6912]{2,1,0:T(1,128)S(1)}, u32[]{:S(2)}, u32[]{:S(2)}) async-start(f32[16,1,6912]{2,1,0:T(1,128)} %reshape.307), calls=%async_computation.3 | async-start | bytes 884736 | tf_op jit(solution)/shard_map/all_to_all | solution.py:81
  249.2 4.4 %copy-start = (f32[4,6,12,192]{3,0,2,1:T(4,128)S(1)}, f32[4,6,12,192]{3,0,2,1:T(4,128)}, u32[]{:S(2)}) copy-start(f32[4,6,12,192]{3,0,2,1:T(4,128)} %param.3) | copy-start | bytes 663556
  249.2 4.4 %copy-start.1 = (f32[6,12,192]{2,1,0:T(8,128)S(1)}, f32[6,12,192]{2,1,0:T(8,128)}, u32[]{:S(2)}) copy-start(f32[6,12,192]{2,1,0:T(8,128)} %param.4) | copy-start | bytes 165892
where the time goes:
time: 371 us; the launch traced here: 366 us
  local copies, waits for them, and re-layouts  131 us (35%)
  blocking collectives  120 us (32%)
  waiting for transfers between devices  52.3 us (14%)
  starting transfers between devices  35.6 us (10%)
  matrix products  16.2 us (4%)
  other arithmetic  10.9 us (3%)
    psum x1, blocking collectives, local(): intersection = lax.psum(partial_intersection, ('slab', 'pencil'))  105 us
    unnamed x14, local copies, waits for them, and re-layouts  63.6 us
    all_to_all x1, waiting for transfers between devices, local(): lax.all_to_all(rows_c, 'pencil', split_axis=4, concat_axis=1, tiled=True)  21.6 us
    all_to_all x1, waiting for transfers between devices, local(): lax.all_to_all(lines_k, 'pencil', split_axis=4, concat_axis=2, tiled=True)  20.2 us
    all_to_all x1, starting transfers between devices, local(): lax.all_to_all(lines_k, 'pencil', split_axis=4, concat_axis=2, tiled=True)  15.9 us
    all_to_all x3, local copies, waits for them, and re-layouts, local(): lax.all_to_all(along_a, 'slab', split_axis=4, concat_axis=2, tiled=True)  14.8 us
    all_to_all x1, blocking collectives, local(): lax.all_to_all(along_a, 'slab', split_axis=4, concat_axis=2, tiled=True)  14.1 us
    all_to_all x1, starting transfers between devices, local(): lax.all_to_all(along_f, 'slab', split_axis=4, concat_axis=1, tiled=True)  14.1 us
  transfers between devices with their start and end apart: 3, of which 3 were waited for; matrix products, arithmetic and copies ran while one was open for 0% of the time, Pallas kernels for 0%

commit v1 on v0

--- a/solution.py
+++ b/solution.py
@@ -9,6 +9,12 @@
 filter_center = 1.0
 filter_half = 1.5
 highest = lax.Precision.HIGHEST
+
+
+def add_all(array, name):
+    parts = lax.all_gather(array, name, axis=0, tiled=False)
+    result = parts.sum(axis=0)
+    return result
 
 
 def frequencies(number, length):
@@ -90,7 +96,7 @@
     number = filtered.shape[0]
     flattened = filtered.reshape(number, -1)
     partial_intersection = jnp.dot(flattened, flattened.T, precision=highest) / float(NG**3)
-    intersection = lax.psum(partial_intersection, ("slab", "pencil"))
+    intersection = add_all(partial_intersection, ("slab", "pencil"))
     factor = jnp.linalg.cholesky(intersection)
     result = jax.scipy.linalg.solve_triangular(factor, flattened, lower=True)
     return result.reshape(filtered.shape)

time: 371 us -> 407 us (1.097)
  the two profiles are of different devices: /device:TPU:1 before, /device:TPU:2 now
where the time goes in v1:
time: 407 us; the launch traced here: 401 us
  blocking collectives  151 us (37%)
  local copies, waits for them, and re-layouts  131 us (32%)
  waiting for transfers between devices  61.7 us (15%)
  starting transfers between devices  29.5 us (7%)
  matrix products  16.2 us (4%)
  other arithmetic  11.5 us (3%)
    all_gather x1, blocking collectives, add_all(): parts = lax.all_gather(array, name, axis=0, tiled=False)  137 us
    unnamed x14, local copies, waits for them, and re-layouts  63.6 us
    all_to_all x1, waiting for transfers between devices, local(): lax.all_to_all(rows_c, 'pencil', split_axis=4, concat_axis=1, tiled=True)  27.1 us
    all_to_all x1, waiting for transfers between devices, local(): lax.all_to_all(lines_k, 'pencil', split_axis=4, concat_axis=2, tiled=True)  25.7 us
    all_to_all x1, starting transfers between devices, local(): lax.all_to_all(lines_k, 'pencil', split_axis=4, concat_axis=2, tiled=True)  15.4 us
    all_to_all x3, local copies, waits for them, and re-layouts, local(): lax.all_to_all(along_a, 'slab', split_axis=4, concat_axis=2, tiled=True)  14.8 us
    all_to_all x1, blocking collectives, local(): lax.all_to_all(along_a, 'slab', split_axis=4, concat_axis=2, tiled=True)  14.1 us
    all_to_all x2, local copies, waits for them, and re-layouts, local(): lax.all_to_all(along_f, 'slab', split_axis=4, concat_axis=1, tiled=True)  12.4 us
  transfers between devices with their start and end apart: 3, of which 3 were waited for; matrix products, arithmetic and copies ran while one was open for 0% of the time, Pallas kernels for 0%

profile of v1, /device:TPU:2, one launch (start us, length us, event | category | flops | bytes accessed | tf_op | source)
XLA Modules:
  0.0 401.4 jit_solution(13529341976312542950)
XLA Ops:
  3.5 3.5 copy.71
  7.0 7.7 %reshape.305 = f32[16,1,6912]{2,1,0:T(1,128)} reshape(f32[192,6,2,4,12]{4,3,2,1,0:T(4,128)} %bitcast.142) | data formatting | bytes 884736
  14.7 15.4 %all-to-all-start = ((f32[16,1,6912]{2,1,0:T(1,128)}), f32[16,1,6912]{2,1,0:T(1,128)S(1)}, u32[]{:S(2)}, u32[]{:S(2)}) async-start(f32[16,1,6912]{2,1,0:T(1,128)} %reshape.305), calls=%async_computation | async-start | bytes 884736 | tf_op jit(solution)/shard_map/all_to_all | solution.py:73
  30.4 25.7 %all-to-all-done = f32[16,1,6912]{2,1,0:T(1,128)S(1)} async-done(((f32[16,1,6912]{2,1,0:T(1,128)}), f32[16,1,6912]{2,1,0:T(1,128)S(1)}, u32[]{:S(2)}, u32[]{:S(2)}) %all-to-all-start) | async-done | bytes 442400 | tf_op jit(solution)/shard_map/all_to_all | solution.py:73
  58.3 7.8 %reshape.306 = f32[192,6,2,4,12]{4,3,2,1,0:T(4,128)} reshape(f32[16,6912]{1,0:T(8,128)S(1)} %reduce.7) | data formatting | bytes 884736
  66.1 7.2 %copy.158 = f32[4,6,12,2,16,12]{2,4,3,5,1,0:T(8,128)} copy(f32[4,6,12,2,16,12]{2,0,3,1,5,4:T(4,128)} %bitcast.143) | data formatting | bytes 884736 | tf_op jit(solution)/shard_map/all_to_all | solution.py:73
  73.3 4.3 %all_to_all.55 = f32[4,6,192,2,12]{2,3,4,1,0:T(2,128)S(1)} reshape(f32[4,6,16,12,2,12]{3,2,4,5,1,0:T(8,128)} %bitcast.144) | data formatting | bytes 884736 | tf_op jit(solution)/shard_map/all_to_all | solution.py:73
  79.1 4.8 %copy.76 = f32[4,6,12,2,192]{2,3,1,0,4:T(2,128)} copy(f32[4,6,12,2,192]{4,2,3,1,0:T(8,128)S(1)} %convolution_bitcast_fusion.3) | data formatting | bytes 884736 | tf_op jit(solution)/shard_map/bacrk,crsf->baksf/dot_general | solution.py:71
  84.0 8.6 %reshape.307 = f32[32,1,3456]{2,1,0:T(1,128)} reshape(f32[192,4,6,2,12]{4,3,2,1,0:T(2,128)} %bitcast.145) | data formatting | bytes 884736
  92.5 8.2 %all-to-all-start.1 = ((f32[32,1,3456]{2,1,0:T(1,128)}), f32[32,1,3456]{2,1,0:T(1,128)S(1)}, u32[]{:S(2)}, u32[]{:S(2)}) async-start(f32[32,1,3456]{2,1,0:T(1,128)} %reshape.307), calls=%async_computation.1 | async-start | bytes 884736 | tf_op jit(solution)/shard_map/all_to_all | solution.py:79
  100.9 8.9 %all-to-all-done.1 = f32[32,1,3456]{2,1,0:T(1,128)S(1)} async-done(((f32[32,1,3456]{2,1,0:T(1,128)}), f32[32,1,3456]{2,1,0:T(1,128)S(1)}, u32[]{:S(2)}, u32[]{:S(2)}) %all-to-all-start.1) | async-done | bytes 442400 | tf_op jit(solution)/shard_map/all_to_all | solution.py:79
  111.5 8.9 %reshape.308 = f32[192,4,6,2,12]{4,3,2,1,0:T(2,128)} reshape(f32[32,3456]{1,0:T(8,128)S(1)} %reduce.8) | data formatting | bytes 884736
  120.4 6.1 %copy.78 = f32[4,32,6,12,2,6]{3,4,5,2,1,0:T(2,128)} copy(f32[4,32,6,12,2,6]{3,4,2,0,5,1:T(2,128)} %bitcast.146) | data formatting | bytes 884736 | tf_op jit(solution)/shard_map/all_to_all | solution.py:79
  126.5 6.3 %copy.103 = f32[4,192,12,2,6,1]{1,4,3,5,2,0:T(8,128)S(1)} copy(f32[4,192,12,2,6,1]{2,3,4,1,0,5:T(2,128)} %bitcast.147) | data formatting | bytes 884736 | tf_op jit(solution)/shard_map/all_to_all | solution.py:79
  132.8 3.0 fusion.1
  135.8 3.0 convolution_bitcast_fusion
  138.8 3.7 copy.82
  142.6 7.2 %reshape.309 = f32[32,1,3456]{2,1,0:T(1,128)S(1)} reshape(f32[192,6,2,4,12]{4,3,2,1,0:T(4,128)} %bitcast.148) | data formatting | bytes 884736
  149.8 14.1 %all_to_all.72 = f32[32,1,3456]{2,1,0:T(1,128)S(1)} all-to-all(f32[32,1,3456]{2,1,0:T(1,128)S(1)} %reshape.309), channel_id=1, replica_groups=mesh['slab'=32,'pencil'=16] {'slab'}, dimensions={0} | all-to-all | bytes 884736 | tf_op jit(solution)/shard_map/all_to_all | solution.py:85
  165.6 7.8 %reshape.310 = f32[192,6,2,4,12]{4,3,2,1,0:T(4,128)} reshape(f32[32,3456]{1,0:T(8,128)S(1)} %reduce.9) | data formatting | bytes 884736
  173.3 4.8 %copy.83 = f32[4,12,6,2,192]{1,3,4,2,0:T(2,128)S(1)} copy(f32[4,12,6,2,192]{1,0,3,2,4:T(4,128)} %bitcast.149) | data formatting | bytes 884736 | tf_op jit(solution)/shard_map/all_to_all | solution.py:85
  178.1 3.7 copy.84
  181.8 6.3 %copy.109 = f32[4,12,192,2,6,1]{2,4,3,5,1,0:T(8,128)S(1)} copy(f32[4,12,192,2,6,1]{1,3,4,2,0,5:T(2,128)} %bitcast.151) | data formatting | bytes 884736 | tf_op jit(solution)/shard_map/all_to_all | solution.py:85
  188.1 3.0 convolution_bitcast_fusion.1
  191.2 3.7 copy.87
  194.9 7.9 %reshape.311 = f32[16,1,6912]{2,1,0:T(1,128)} reshape(f32[192,6,2,4,12]{4,3,2,1,0:T(4,128)} %bitcast.152) | data formatting | bytes 884736
  202.8 5.9 %all-to-all-start.3 = ((f32[16,1,6912]{2,1,0:T(1,128)}), f32[16,1,6912]{2,1,0:T(1,128)S(1)}, u32[]{:S(2)}, u32[]{:S(2)}) async-start(f32[16,1,6912]{2,1,0:T(1,128)} %reshape.311), calls=%async_computation.3 | async-start | bytes 884736 | tf_op jit(solution)/shard_map/all_to_all | solution.py:87
  208.7 27.1 %all-to-all-done.3 = f32[16,1,6912]{2,1,0:T(1,128)S(1)} async-done(((f32[16,1,6912]{2,1,0:T(1,128)}), f32[16,1,6912]{2,1,0:T(1,128)S(1)}, u32[]{:S(2)}, u32[]{:S(2)}) %all-to-all-start.3) | async-done | bytes 442400 | tf_op jit(solution)/shard_map/all_to_all | solution.py:87
  237.5 7.8 %reshape.312 = f32[192,6,2,4,12]{4,3,2,1,0:T(4,128)} reshape(f32[16,6912]{1,0:T(8,128)S(1)} %reduce.10) | data formatting | bytes 884736
  245.3 7.2 %copy.157 = f32[4,12,6,2,16,12]{1,4,3,5,2,0:T(8,128)} copy(f32[4,12,6,2,16,12]{1,0,3,2,5,4:T(4,128)} %bitcast.153) | data formatting | bytes 884736 | tf_op jit(solution)/shard_map/all_to_all | solution.py:87
  252.5 4.4 %all_to_all.67 = f32[4,192,6,2,12]{1,3,4,2,0:T(2,128)S(1)} reshape(f32[4,16,12,6,2,12]{2,1,4,5,3,0:T(8,128)} %bitcast.154) | data formatting | bytes 884736 | tf_op jit(solution)/shard_map/all_to_all | solution.py:87
  259.5 137.0 %all-gather.1 = f32[512,4,4]{2,1,0:T(4,128)S(1)} all-gather(f32[1,4,4]{2,1,0:T(4,128)S(1)} %fusion.8), channel_id=2, replica_groups=mesh['slab'=32,'pencil'=16] {'slab','pencil'}, dimensions={0}, use_global_device_ids=true | all-gather | bytes 32832 | tf_op jit(solution)/shard_map/all_gather | solution.py:15
  (35 shorter events, 19.6 us)
Async XLA Ops:
  14.7 41.4 %all-to-all-start = ((f32[16,1,6912]{2,1,0:T(1,128)}), f32[16,1,6912]{2,1,0:T(1,128)S(1)}, u32[]{:S(2)}, u32[]{:S(2)}) async-start(f32[16,1,6912]{2,1,0:T(1,128)} %reshape.305), calls=%async_computation | async-start | bytes 884736 | tf_op jit(solution)/shard_map/all_to_all | solution.py:73
  92.5 17.2 %all-to-all-start.1 = ((f32[32,1,3456]{2,1,0:T(1,128)}), f32[32,1,3456]{2,1,0:T(1,128)S(1)}, u32[]{:S(2)}, u32[]{:S(2)}) async-start(f32[32,1,3456]{2,1,0:T(1,128)} %reshape.307), calls=%async_computation.1 | async-start | bytes 884736 | tf_op jit(solution)/shard_map/all_to_all | solution.py:79
  191.1 17.5 %copy-start.2 = (s32[4]{0:T(128)S(1)}, s32[4]{0:T(128)}, u32[]{:S(2)}) copy-start(s32[4]{0:T(128)} %param.5) | copy-start | bytes 52
  202.8 33.0 %all-to-all-start.3 = ((f32[16,1,6912]{2,1,0:T(1,128)}), f32[16,1,6912]{2,1,0:T(1,128)S(1)}, u32[]{:S(2)}, u32[]{:S(2)}) async-start(f32[16,1,6912]{2,1,0:T(1,128)} %reshape.311), calls=%async_computation.3 | async-start | bytes 884736 | tf_op jit(solution)/shard_map/all_to_all | solution.py:87
  252.5 4.4 %copy-start = (f32[4,6,12,192]{3,0,2,1:T(4,128)S(1)}, f32[4,6,12,192]{3,0,2,1:T(4,128)}, u32[]{:S(2)}) copy-start(f32[4,6,12,192]{3,0,2,1:T(4,128)} %param.3) | copy-start | bytes 663556
  252.5 4.4 %copy-start.1 = (f32[6,12,192]{2,1,0:T(8,128)S(1)}, f32[6,12,192]{2,1,0:T(8,128)}, u32[]{:S(2)}) copy-start(f32[6,12,192]{2,1,0:T(8,128)} %param.4) | copy-start | bytes 165892
